TPU v7x, 32 devices: a whole 2x2x4 slice. The times are simulated.
32 devices in a mesh: groups: 2 (over x), ctx: 16 (over z, y, core).
Axes of the slice: x: 2, y: 2, z: 4, core: 2. Of those that a mesh axis runs over, the one named last changes fastest.
Arguments:
- q_latent: bfloat16 [128, 1536], P(('groups', 'ctx')), parts along dimension 0, may hold values from -64 to 64
- q_gain: float32 [1536], replicated, may hold values from 0.1 to 1.9
- w_uq: bfloat16 [1536, 24576], P(None, 'ctx'), may hold values from -0.15625 to 0.15625
- w_uk: bfloat16 [128, 128, 512], P('ctx'), may hold values from -0.5 to 0.5
- w_uv: bfloat16 [128, 512, 128], P('ctx'), may hold values from -0.25 to 0.25
- w_o: bfloat16 [16384, 7168], P('ctx'), may hold values from -0.046875 to 0.046875
- latent_cache: bfloat16 [65536, 576], P(('groups', 'ctx')), parts along dimension 0, may hold values from -1024 to 1024
- kv_scales: float32 [65536, 4], P(('groups', 'ctx')), parts along dimension 0, may hold values from 0.5 to 2
- selected: int32 [128, 32], P(('groups', 'ctx')), parts along dimension 0, may hold values from 0 to 511, as said below
- counts: int32 [128], P(('groups', 'ctx')), parts along dimension 0, may hold values from 8 to 32
Outputs:
- attn_out: bfloat16 [128, 7168], P(('groups', 'ctx')), parts along dimension 0
There are 2 independent parts, one for each index of `groups`. A program takes and returns all parts, laid end to end along the dimension named above; an argument that names none is the same for every part. Nothing has to cross between parts.
Inputs may be any that keep to these rules, and one draw needn't show every extreme that they name: `selected`: each row lists 32 different block numbers. Over the rows 4 i to 4 i + 4 - 1 (the query tokens of one device) and their first counts entries, at most 8 different listed blocks lie in the range 32 j to 32 j + 31 for any j.
All inputs are finite; a program needn't handle non-finite values.
Results may differ from a plain program's by a relative error of at most 0.01.
The roundings to bfloat16 on the way count: a program that leaves them out, or rounds other values in their place, can miss the bound.
Values may be sent and summed in bfloat16 or wider, within the bound.
A program may use at most 128 MiB of HBM per device.

v0:
```python
import math
import jax
import jax.numpy as jnp
from jax import lax
from jax.sharding import PartitionSpec as P

BLK = 64
norm_eps = 1e-06
rope_base = 10000.0


def rotate_rotary(rotary, positions):
    half_width = rotary.shape[-1] // 2
    freq_index = jnp.arange(half_width, dtype=jnp.float32)
    inverse_freq = jnp.exp(freq_index * (-2.0 * math.log(rope_base) / rotary.shape[-1]))
    angles = positions[:, None] * inverse_freq[None, :]
    cosine = jnp.cos(angles)[:, None, :]
    sine = jnp.sin(angles)[:, None, :]
    first_half = rotary[:, :, :half_width]
    second_half = rotary[:, :, half_width:]
    return jnp.concatenate(
        [first_half * cosine - second_half * sine, first_half * sine + second_half * cosine], axis=2
    )


def local(q_latent, q_gain, w_uq, w_uk, w_uv, w_o, latent_cache, kv_scales, selected, counts):
    n_devices = lax.axis_size("ctx")
    heads_local = w_uk.shape[0]
    width_content = w_uk.shape[1]
    width_latent = w_uk.shape[2]
    width_rotary = latent_cache.shape[1] - width_latent
    width_row = width_latent + width_rotary
    q_local = q_latent.shape[0]
    top_blocks = selected.shape[1]
    block_len = BLK
    blocks_local = latent_cache.shape[0] // block_len
    blocks_total = blocks_local * n_devices
    capacity = max(2, 4 * top_blocks // n_devices)
    latent_f = q_latent.astype(jnp.float32)
    normed = (
        latent_f
        * lax.rsqrt(jnp.mean(latent_f * latent_f, axis=1, keepdims=True) + norm_eps)
        * q_gain
    ).astype(jnp.bfloat16)
    scaled = (
        latent_cache[:, :width_latent].astype(jnp.float32)
        * jnp.repeat(kv_scales, width_latent // kv_scales.shape[1], axis=1)
    ).astype(jnp.bfloat16)
    cache_blocks = jnp.concatenate([scaled, latent_cache[:, width_latent:]], axis=1).reshape(
        blocks_local, block_len, width_row
    )
    live_sel = jnp.arange(top_blocks, dtype=jnp.int32)[None, :] < counts[:, None]
    block_match = selected[:, :, None] == jnp.arange(blocks_total, dtype=jnp.int32)[None, None, :]
    needed = (
        jnp.any(block_match & live_sel[:, :, None], axis=(0, 1))
        .reshape(n_devices, blocks_local)
        .astype(jnp.int32)
    )
    order_rank = jnp.cumsum(needed, axis=1) - 1
    slot_match = (needed[:, :, None] == 1) & (
        order_rank[:, :, None] == jnp.arange(capacity, dtype=jnp.int32)[None, None, :]
    )
    requests = jnp.sum(
        jnp.where(slot_match, jnp.arange(blocks_local, dtype=jnp.int32)[None, :, None], 0), axis=1
    )
    rank_flat = order_rank.reshape(blocks_total)
    sel_rank = jnp.sum(jnp.where(block_match, rank_flat[None, None, :], 0), axis=2)
    slot_index = jnp.where(live_sel, selected // blocks_local * capacity + sel_rank, 0)
    shard_piece = lax.all_gather(normed, "ctx", axis=0, tiled=True)
    row_count = shard_piece.shape[0]
    projected = jnp.dot(shard_piece, w_uq, preferred_element_type=jnp.float32).reshape(
        row_count, heads_local, width_content + width_rotary
    )
    content = projected[:, :, :width_content].astype(jnp.bfloat16)
    positions = jnp.arange(row_count, dtype=jnp.int32).astype(jnp.float32)
    rotated = rotate_rotary(projected[:, :, width_content:], positions).astype(jnp.bfloat16)
    absorbed = jnp.einsum("khn,hnc->khc", content, w_uk, preferred_element_type=jnp.float32).astype(
        jnp.bfloat16
    )
    head_queries = jnp.concatenate([absorbed, rotated], axis=2)
    queries = lax.all_to_all(head_queries, "ctx", split_axis=0, concat_axis=1, tiled=True)
    served = cache_blocks[lax.all_to_all(requests, "ctx", split_axis=0, concat_axis=0, tiled=True)]
    fetched = lax.all_to_all(served, "ctx", split_axis=0, concat_axis=0, tiled=True)
    fetched_rows = fetched.reshape(n_devices * capacity * block_len, width_row)
    token_index = (
        slot_index[:, :, None] * block_len + jnp.arange(block_len, dtype=jnp.int32)[None, None, :]
    ).reshape(q_local, top_blocks * block_len)
    live_tokens = jnp.repeat(live_sel, block_len, axis=1)
    softmax_scale = 1.0 / math.sqrt(width_content + width_rotary)

    def attend(inputs):
        query_row, token_rows, live_row = inputs
        key_rows = fetched_rows[token_rows]
        scores = jnp.dot(query_row, key_rows.T, preferred_element_type=jnp.float32) * softmax_scale
        scores = jnp.where(live_row[None, :], scores, -jnp.inf)
        row_peak = jnp.max(scores, axis=1, keepdims=True)
        exponent = jnp.exp(scores - row_peak)
        weights = (exponent / jnp.sum(exponent, axis=1, keepdims=True)).astype(jnp.bfloat16)
        return jnp.dot(
            weights, key_rows[:, :width_latent], preferred_element_type=jnp.float32
        ).astype(jnp.bfloat16)

    latent_out = lax.map(attend, (queries, token_index, live_tokens))
    head_out = lax.all_to_all(latent_out, "ctx", split_axis=1, concat_axis=0, tiled=True)
    head_values = jnp.einsum(
        "qhc,hcv->qhv", head_out, w_uv, preferred_element_type=jnp.float32
    ).astype(jnp.bfloat16)
    head_values = head_values.reshape(head_values.shape[0], heads_local * w_uv.shape[2])
    return lax.psum_scatter(
        jnp.dot(head_values, w_o, preferred_element_type=jnp.float32),
        "ctx",
        scatter_dimension=0,
        tiled=True,
    ).astype(jnp.bfloat16)


def solution(mesh):
    in_specs = (
        P(("groups", "ctx"), None),
        P(),
        P(None, "ctx"),
        P("ctx", None, None),
        P("ctx", None, None),
        P("ctx", None),
        P(("groups", "ctx"), None),
        P(("groups", "ctx"), None),
        P(("groups", "ctx"), None),
        P(("groups", "ctx")),
    )
    out_specs = P(("groups", "ctx"), None)
    return jax.shard_map(local, mesh=mesh, in_specs=in_specs, out_specs=out_specs, check_vma=False)
```

profile of v0, /device:TPU:0, one launch (start us, length us, event | category | flops | bytes accessed | tf_op | source)
XLA Modules:
  0.0 466.6 jit_solution(13454047989507777395)
XLA Ops:
  0.0 0.8 iota_compare_fusion.2
  0.8 0.8 fusion.22
  1.6 0.1 reshape.195
  1.7 0.2 reduce_window_sum.11
  1.9 1.0 select_reduce_fusion.1
  2.9 7.4 %all-to-all-start.1 = ((s32[16,1,8]{2,1,0:T(1,128)}), s32[16,1,8]{2,1,0:T(1,128)S(1)}, u32[]{:S(2)}, u32[]{:S(2)}) async-start(s32[16,1,8]{2,1,0:T(1,128)} %bitcast.18), calls=%async_computation.1 | async-start | bytes 16384 | tf_op jit(solution)/shard_map/all_to_all | solution.py:82
  10.3 0.8 fusion.27
  11.2 0.8 fusion.30
  12.0 22.2 %all-gather = bf16[16,4,1536]{2,1,0:T(4,128)(2,1)S(1)} all-gather(bf16[1,4,1536]{2,1,0:T(4,128)(2,1)S(1)} %fusion.30), channel_id=1, replica_groups=mesh['groups'=2,'ctx'=16] {'ctx'}, dimensions={0}, use_global_device_ids=true | all-gather | bytes 208896 | tf_op jit(solution)/shard_map/all_gather | solution.py:69
  34.2 3.3 fusion.39
  37.5 0.2 reshape.190
  37.7 0.1 fusion.38
  37.8 0.2 multiply_cosine_fusion
  38.0 0.3 fusion.19
  38.3 0.1 subtract_convert_fusion
  38.5 0.1 pad_maximum_fusion.1
  38.6 1.2 copy.45
  39.8 0.4 copy.48
  40.2 0.2 slice-done
  40.4 2.5 copy.59
  42.9 1.0 copy.60
  44.0 4.3 all-to-all-start
  48.2 4.7 %broadcast_in_dim.79 = f32[2048,4,128]{2,1,0:T(4,128)S(1)} broadcast(f32[2048,4]{1,0:T(8,128)S(1)} %copy.48), dimensions={0,1} | broadcast | bytes 4227072 | tf_op jit(solution)/shard_map/broadcast_in_dim | solution.py:47
  52.9 1.0 fusion.18
  54.0 0.2 pad_maximum_fusion
  54.4 0.1 reshape.206
  54.5 7.6 %gather_fusion.1 = bf16[128,64,576]{2,1,0:T(8,128)(2,1)} fusion(bf16[32,64,576]{2,1,0:T(8,128)(2,1)S(1)} %bitcast.67, s32[1024]{0:T(1024)S(1)} %pad_clamp_fusion), kind=kCustom, calls=%fused_computation.1 | custom fusion | bytes 18874880 | tf_op jit(solution)/shard_map/gather | solution.py:82
  62.1 2.7 all-to-all-done
  64.8 5.1 %all-to-all-start.2 = ((bf16[16,8,64,576]{3,2,1,0:T(8,128)(2,1)}), bf16[16,8,64,576]{3,2,1,0:T(8,128)(2,1)}, u32[]{:S(2)}, u32[]{:S(2)}) async-start(bf16[16,8,64,576]{3,2,1,0:T(8,128)(2,1)} %bitcast.68), calls=%async_computation.2 | async-start | bytes 20971520 | tf_op jit(solution)/shard_map/all_to_all | solution.py:83
  70.0 0.1 sub.26
  70.0 0.2 select_reduce_fusion
  70.4 0.1 add.76
  70.4 0.1 add.77
  70.6 0.1 broadcast_in_dim.50
  70.7 0.1 reshape.189
  70.8 1.1 copy.79
  72.0 184.8 %all-to-all-done.2 = bf16[16,8,64,576]{3,2,1,0:T(8,128)(2,1)} async-done(((bf16[16,8,64,576]{3,2,1,0:T(8,128)(2,1)}), bf16[16,8,64,576]{3,2,1,0:T(8,128)(2,1)}, u32[]{:S(2)}, u32[]{:S(2)}) %all-to-all-start.2) | async-done | bytes 9437216 | tf_op jit(solution)/shard_map/all_to_all | solution.py:83
  256.8 63.6 %while.10 = (s32[]{:T(128)}, bf16[4,128,512]{2,1,0:T(8,128)(2,1)}, pred[4,2048]{1,0:T(4,128)(4,1)S(1)}, bf16[4,128,576]{2,1,0:T(8,128)(2,1)S(1)}, s32[4,2048]{1,...) while((s32[]{:T(128)}, bf16[4,128,512]{2,1,0:T(8,128)(2,1)}, pred[4,2048]{1,0:T(4,128)(4,1)S(1)}, ...), condition=%wide.region_8.9_spmd, body=%wide.region_5.8_spmd.sunk | while | flops 572595968 | bytes 12928089 | solution.py:103
  256.8 13.3 %gather_fusion = bf16[2048,576]{1,0:T(8,128)(2,1)S(1)} fusion(bf16[8192,576]{1,0:T(8,128)(2,1)} %get-tuple-element.118, s32[2048]{0:T(1024)S(1)} %broadcast_clamp_fusion.2), kind=kCustom, calls=%fused_computation.clone.1 | custom fusion | bytes 4726784 | tf_op jit(solution)/shard_map/while/body/eval_jaxpr/gather | solution.py:93
  270.2 1.1 fusion.54
  271.2 0.3 fusion.55
  271.5 1.2 fusion.56
  272.8 13.3 %gather_fusion = bf16[2048,576]{1,0:T(8,128)(2,1)S(1)} fusion(bf16[8192,576]{1,0:T(8,128)(2,1)} %get-tuple-element.118, s32[2048]{0:T(1024)S(1)} %broadcast_clamp_fusion.2), kind=kCustom, calls=%fused_computation.clone.1 | custom fusion | bytes 4726784 | tf_op jit(solution)/shard_map/while/body/eval_jaxpr/gather | solution.py:93
  286.1 1.1 fusion.54
  287.2 0.3 fusion.55
  287.5 1.2 fusion.56
  288.7 13.3 %gather_fusion = bf16[2048,576]{1,0:T(8,128)(2,1)S(1)} fusion(bf16[8192,576]{1,0:T(8,128)(2,1)} %get-tuple-element.118, s32[2048]{0:T(1024)S(1)} %broadcast_clamp_fusion.2), kind=kCustom, calls=%fused_computation.clone.1 | custom fusion | bytes 4726784 | tf_op jit(solution)/shard_map/while/body/eval_jaxpr/gather | solution.py:93
  302.0 1.1 fusion.54
  303.1 0.3 fusion.55
  303.4 1.2 fusion.56
  304.6 13.3 %gather_fusion = bf16[2048,576]{1,0:T(8,128)(2,1)S(1)} fusion(bf16[8192,576]{1,0:T(8,128)(2,1)} %get-tuple-element.118, s32[2048]{0:T(1024)S(1)} %broadcast_clamp_fusion.2), kind=kCustom, calls=%fused_computation.clone.1 | custom fusion | bytes 4726784 | tf_op jit(solution)/shard_map/while/body/eval_jaxpr/gather | solution.py:93
  317.9 1.1 fusion.54
  319.0 0.3 fusion.55
  319.3 1.2 fusion.56
  320.4 2.3 copy.54
  322.8 45.6 %all-to-all-start.3 = ((bf16[4,128,512]{2,0,1:T(4,128)(2,1)}), bf16[4,128,512]{2,0,1:T(4,128)(2,1)S(1)}, u32[]{:S(2)}, u32[]{:S(2)}) async-start(bf16[4,128,512]{2,0,1:T(4,128)(2,1)} %copy.54), calls=%async_computation.3 | async-start | bytes 1048576 | tf_op jit(solution)/shard_map/all_to_all | solution.py:104
  368.4 0.6 dynamic-slice
  369.7 13.0 %all-to-all-done.3 = bf16[4,128,512]{2,0,1:T(4,128)(2,1)S(1)} async-done(((bf16[4,128,512]{2,0,1:T(4,128)(2,1)}), bf16[4,128,512]{2,0,1:T(4,128)(2,1)S(1)}, u32[]{:S(2)}, u32[]{:S(2)}) %all-to-all-start.3) | async-done | bytes 524320 | tf_op jit(solution)/shard_map/all_to_all | solution.py:104
  382.7 0.2 copy.80
  382.9 0.1 all_to_all.48
  383.0 0.3 fusion.20
  383.3 8.0 %fusion.23 = f32[64,7168]{1,0:T(8,128)S(1)} fusion(bf16[1024,7168]{1,0:T(8,128)(2,1)} %param.17, bf16[8,8,8,128]{3,2,1,0:T(8,128)(2,1)S(1)} %fusion.20), kind=kOutput, calls=%fused_computation.37 | convolution fusion | flops 939524096 | bytes 16646144 | tf_op jit(solution)/shard_map/dot_general | solution.py:110
  391.3 73.7 %all-reduce.2 = bf16[64,7168]{1,0:T(8,128)(2,1)} all-reduce(f32[64,7168]{1,0:T(8,128)S(1)} %fusion.23), channel_id=2, replica_groups=mesh['groups'=2,'ctx'=16] {'ctx'}, use_global_device_ids=true, to_apply=%region_9.10.clone | all-reduce | flops 458752 | bytes 2752512
  465.1 1.6 dynamic-slice_convert_fusion
  (51 shorter events, 0.8 us)
Async XLA Ops:
  0.0 38.0 %copy-start = (bf16[8,128,512]{2,1,0:T(8,128)(2,1)S(1)}, bf16[8,128,512]{2,1,0:T(8,128)(2,1)}, u32[]{:S(2)}) copy-start(bf16[8,128,512]{2,1,0:T(8,128)(2,1)} %param.15) | copy-start | bytes 3145732
  2.9 41.1 %all-to-all-start.1 = ((s32[16,1,8]{2,1,0:T(1,128)}), s32[16,1,8]{2,1,0:T(1,128)S(1)}, u32[]{:S(2)}, u32[]{:S(2)}) async-start(s32[16,1,8]{2,1,0:T(1,128)} %bitcast.18), calls=%async_computation.1 | async-start | bytes 16384 | tf_op jit(solution)/shard_map/all_to_all | solution.py:82
  38.6 1.2 copy-start.5
  38.6 1.8 slice-start
  39.8 3.1 slice-start.1
  44.0 20.9 %all-to-all-start = ((bf16[64,8,576]{2,1,0:T(8,128)(2,1)}), bf16[64,8,576]{2,1,0:T(8,128)(2,1)}, u32[]{:S(2)}, u32[]{:S(2)}) async-start(bf16[64,8,576]{2,1,0:T(8,128)(2,1)} %copy.45), calls=%async_computation | async-start | bytes 1310720 | tf_op jit(solution)/shard_map/all_to_all | solution.py:81
  48.2 4.7 %copy-start.2 = (bf16[2048,512]{1,0:T(8,128)(2,1)S(1)}, bf16[2048,512]{1,0:T(8,128)(2,1)}, u32[]{:S(2)}) copy-start(bf16[2048,512]{1,0:T(8,128)(2,1)} %copy.59) | copy-start | bytes 6291460
  52.9 1.0 copy-start.3
  64.8 5.2 %copy-start.6 = (s32[4,32]{1,0:T(4,128)S(1)}, s32[4,32]{1,0:T(4,128)}, u32[]{:S(2)}) copy-start(s32[4,32]{1,0:T(4,128)} %param.20) | copy-start | bytes 1540
  64.8 5.5 %copy-start.7 = (s32[4]{0:T(128)S(1)}, s32[4]{0:T(128)}, u32[]{:S(2)}) copy-start(s32[4]{0:T(128)} %param.21) | copy-start | bytes 52
  64.8 192.0 %all-to-all-start.2 = ((bf16[16,8,64,576]{3,2,1,0:T(8,128)(2,1)}), bf16[16,8,64,576]{3,2,1,0:T(8,128)(2,1)}, u32[]{:S(2)}, u32[]{:S(2)}) async-start(bf16[16,8,64,576]{3,2,1,0:T(8,128)(2,1)} %bitcast.68), calls=%async_computation.2 | async-start | bytes 20971520 | tf_op jit(solution)/shard_map/all_to_all | solution.py:83
  256.8 111.6 %copy-start.8 = (u32[32]{0:T(128)S(1)}, u32[32]{0:T(128)}, u32[]{:S(2)}) copy-start(u32[32]{0:T(128)} %constant.72) | copy-start | bytes 388
  320.4 62.6 %copy-start.4 = (bf16[8,512,128]{2,1,0:T(8,128)(2,1)S(1)}, bf16[8,512,128]{2,1,0:T(8,128)(2,1)}, u32[]{:S(2)}) copy-start(bf16[8,512,128]{2,1,0:T(8,128)(2,1)} %param.16) | copy-start | bytes 3145732
  322.8 59.9 %all-to-all-start.3 = ((bf16[4,128,512]{2,0,1:T(4,128)(2,1)}), bf16[4,128,512]{2,0,1:T(4,128)(2,1)S(1)}, u32[]{:S(2)}, u32[]{:S(2)}) async-start(bf16[4,128,512]{2,0,1:T(4,128)(2,1)} %copy.54), calls=%async_computation.3 | async-start | bytes 1048576 | tf_op jit(solution)/shard_map/all_to_all | solution.py:104
  383.3 83.3 %copy-start.1 = (bf16[8,128,512]{2,1,0:T(8,128)(2,1)S(1)}, bf16[8,128,512]{2,1,0:T(8,128)(2,1)}, u32[]{:S(2)}) copy-start(bf16[8,128,512]{2,1,0:T(8,128)(2,1)} %param.15) | copy-start | bytes 3145732
where the time goes:
time: 468 us; the launch traced here: 467 us
  waiting for transfers between devices  201 us (43%)
  blocking collectives  95.9 us (20%)
  local copies, waits for them, and re-layouts  78.1 us (17%)
  starting transfers between devices  62.5 us (13%)
  matrix products  20.8 us (4%)
  other arithmetic  7.66 us (2%)
    all_to_all x1, waiting for transfers between devices, local(): lax.all_to_all(served, 'ctx', split_axis=0, concat_axis=0, tiled=True)  185 us
    unnamed x1, blocking collectives  73.7 us
    gather x4, local copies, waits for them, and re-layouts, attend(): key_rows = fetched_rows[token_rows]  53.1 us
    all_to_all x1, starting transfers between devices, local(): lax.all_to_all(latent_out, 'ctx', split_axis=1, concat_axis=0, tiled=True)  45.6 us
    all_gather x1, blocking collectives, local(): shard_piece = lax.all_gather(normed, 'ctx', axis=0, tiled=True)  22.2 us
    all_to_all x1, waiting for transfers between devices, local(): lax.all_to_all(latent_out, 'ctx', split_axis=1, concat_axis=0, tiled=True)  13 us
  transfers between devices with their start and end apart: 4, of which 3 were waited for; matrix products, arithmetic and copies ran while one was open for 6% of the time, Pallas kernels for 0%

commit v1 on v0

--- a/solution.py
+++ b/solution.py
@@ -3,6 +3,7 @@
 import jax.numpy as jnp
 from jax import lax
 from jax.sharding import PartitionSpec as P
+from jax.lax import all_to_all, axis_size
 
 BLK = 64
 norm_eps = 1e-06
@@ -24,6 +25,12 @@
 
 
 def local(q_latent, q_gain, w_uq, w_uk, w_uv, w_o, latent_cache, kv_scales, selected, counts):
+
+    def cut_the_spans(frame):
+        return jnp.concatenate(
+            all_to_all(jnp.stack(jnp.split(frame, axis_size("ctx"), axis=1)), "ctx", 0, 0), axis=0
+        )
+
     n_devices = lax.axis_size("ctx")
     heads_local = w_uk.shape[0]
     width_content = w_uk.shape[1]
@@ -101,7 +108,7 @@
         ).astype(jnp.bfloat16)
 
     latent_out = lax.map(attend, (queries, token_index, live_tokens))
-    head_out = lax.all_to_all(latent_out, "ctx", split_axis=1, concat_axis=0, tiled=True)
+    head_out = cut_the_spans(latent_out)
     head_values = jnp.einsum(
         "qhc,hcv->qhv", head_out, w_uv, preferred_element_type=jnp.float32
     ).astype(jnp.bfloat16)

time: 468 us -> 489 us (1.045)
  local copies, waits for them, and re-layouts: 78.1 us -> 97.3 us
    unnamed x23 -> x36, local copies, waits for them, and re-layouts: 4.63 us -> 25 us
where the time goes in v1:
time: 489 us; the launch traced here: 487 us
  waiting for transfers between devices  201 us (41%)
  local copies, waits for them, and re-layouts  97.3 us (20%)
  blocking collectives  95.9 us (20%)
  starting transfers between devices  62.5 us (13%)
  matrix products  22.1 us (5%)
  other arithmetic  7.66 us (2%)
    all_to_all x1, waiting for transfers between devices, local(): lax.all_to_all(served, 'ctx', split_axis=0, concat_axis=0, tiled=True)  185 us
    unnamed x1, blocking collectives  73.7 us
    gather x4, local copies, waits for them, and re-layouts, attend(): key_rows = fetched_rows[token_rows]  53.1 us
    all_to_all x1, starting transfers between devices, cut_the_spans(): all_to_all(jnp.stack(jnp.split(frame, axis_size('ctx'), axis=1)), 'ctx',...  45.6 us
    unnamed x36, local copies, waits for them, and re-layouts  25 us
    all_gather x1, blocking collectives, local(): shard_piece = lax.all_gather(normed, 'ctx', axis=0, tiled=True)  22.2 us
    all_to_all x1, waiting for transfers between devices, cut_the_spans(): all_to_all(jnp.stack(jnp.split(frame, axis_size('ctx'), axis=1)), 'ctx',...  13 us
  transfers between devices with their start and end apart: 4, of which 3 were waited for; matrix products, arithmetic and copies ran while one was open for 6% of the time, Pallas kernels for 0%

profile of v1, /device:TPU:0, one launch (start us, length us, event | category | flops | bytes accessed | tf_op | source)
XLA Modules:
  0.0 487.0 jit_solution(8213288325836384564)
XLA Ops:
  0.0 0.8 iota_compare_fusion.2
  0.8 0.8 fusion.23
  1.9 1.0 select_reduce_fusion.1
  2.9 7.4 %all-to-all-start.1 = ((s32[16,1,8]{2,1,0:T(1,128)}), s32[16,1,8]{2,1,0:T(1,128)S(1)}, u32[]{:S(2)}, u32[]{:S(2)}) async-start(s32[16,1,8]{2,1,0:T(1,128)} %bitcast.33), calls=%async_computation.1 | async-start | bytes 16384 | tf_op jit(solution)/shard_map/all_to_all | solution.py:89
  10.3 0.8 fusion.28
  11.2 0.8 fusion.31
  12.0 22.2 %all-gather = bf16[16,4,1536]{2,1,0:T(4,128)(2,1)S(1)} all-gather(bf16[1,4,1536]{2,1,0:T(4,128)(2,1)S(1)} %fusion.31), channel_id=1, replica_groups=mesh['groups'=2,'ctx'=16] {'ctx'}, dimensions={0}, use_global_device_ids=true | all-gather | bytes 208896 | tf_op jit(solution)/shard_map/all_gather | solution.py:76
  34.2 3.3 fusion.40
  38.0 0.3 fusion.19
  38.6 1.2 copy.44
  39.8 0.4 copy.47
  40.2 0.2 slice-done
  40.4 2.5 copy.58
  42.9 1.0 copy.59
  44.0 4.3 all-to-all-start
  48.2 4.7 broadcast_in_dim.79
  52.9 1.0 fusion.18
  54.0 0.2 pad_maximum_fusion
  54.5 7.6 %gather_fusion.1 = bf16[128,64,576]{2,1,0:T(8,128)(2,1)} fusion(bf16[32,64,576]{2,1,0:T(8,128)(2,1)S(1)} %bitcast.93, s32[1024]{0:T(1024)S(1)} %pad_clamp_fusion), kind=kCustom, calls=%fused_computation.1 | custom fusion | bytes 18874880 | tf_op jit(solution)/shard_map/gather | solution.py:89
  62.1 2.7 all-to-all-done
  64.8 5.1 %all-to-all-start.2 = ((bf16[16,8,64,576]{3,2,1,0:T(8,128)(2,1)}), bf16[16,8,64,576]{3,2,1,0:T(8,128)(2,1)}, u32[]{:S(2)}, u32[]{:S(2)}) async-start(bf16[16,8,64,576]{3,2,1,0:T(8,128)(2,1)} %bitcast.94), calls=%async_computation.2 | async-start | bytes 20971520 | tf_op jit(solution)/shard_map/all_to_all | solution.py:90
  70.0 0.2 select_reduce_fusion
  70.8 1.1 copy.79
  72.0 184.8 %all-to-all-done.2 = bf16[16,8,64,576]{3,2,1,0:T(8,128)(2,1)} async-done(((bf16[16,8,64,576]{3,2,1,0:T(8,128)(2,1)}), bf16[16,8,64,576]{3,2,1,0:T(8,128)(2,1)}, u32[]{:S(2)}, u32[]{:S(2)}) %all-to-all-start.2) | async-done | bytes 9437216 | tf_op jit(solution)/shard_map/all_to_all | solution.py:90
  256.8 63.6 %while.10 = (s32[]{:T(128)}, bf16[4,128,512]{2,1,0:T(8,128)(2,1)}, pred[4,2048]{1,0:T(4,128)(4,1)S(1)}, bf16[4,128,576]{2,1,0:T(8,128)(2,1)S(1)}, s32[4,2048]{1,...) while((s32[]{:T(128)}, bf16[4,128,512]{2,1,0:T(8,128)(2,1)}, pred[4,2048]{1,0:T(4,128)(4,1)S(1)}, ...), condition=%wide.region_8.9_spmd, body=%wide.region_5.8_spmd.sunk | while | flops 572595968 | bytes 12928089 | solution.py:110
  256.8 13.3 %gather_fusion = bf16[2048,576]{1,0:T(8,128)(2,1)S(1)} fusion(bf16[8192,576]{1,0:T(8,128)(2,1)} %get-tuple-element.118, s32[2048]{0:T(1024)S(1)} %broadcast_clamp_fusion.2), kind=kCustom, calls=%fused_computation.clone.1 | custom fusion | bytes 4726784 | tf_op jit(solution)/shard_map/while/body/eval_jaxpr/gather | solution.py:100
  270.2 1.1 fusion.54
  271.2 0.3 fusion.55
  271.5 1.2 fusion.56
  272.8 13.3 %gather_fusion = bf16[2048,576]{1,0:T(8,128)(2,1)S(1)} fusion(bf16[8192,576]{1,0:T(8,128)(2,1)} %get-tuple-element.118, s32[2048]{0:T(1024)S(1)} %broadcast_clamp_fusion.2), kind=kCustom, calls=%fused_computation.clone.1 | custom fusion | bytes 4726784 | tf_op jit(solution)/shard_map/while/body/eval_jaxpr/gather | solution.py:100
  286.1 1.1 fusion.54
  287.2 0.3 fusion.55
  287.5 1.2 fusion.56
  288.7 13.3 %gather_fusion = bf16[2048,576]{1,0:T(8,128)(2,1)S(1)} fusion(bf16[8192,576]{1,0:T(8,128)(2,1)} %get-tuple-element.118, s32[2048]{0:T(1024)S(1)} %broadcast_clamp_fusion.2), kind=kCustom, calls=%fused_computation.clone.1 | custom fusion | bytes 4726784 | tf_op jit(solution)/shard_map/while/body/eval_jaxpr/gather | solution.py:100
  302.0 1.1 fusion.54
  303.1 0.3 fusion.55
  303.4 1.2 fusion.56
  304.6 13.3 %gather_fusion = bf16[2048,576]{1,0:T(8,128)(2,1)S(1)} fusion(bf16[8192,576]{1,0:T(8,128)(2,1)} %get-tuple-element.118, s32[2048]{0:T(1024)S(1)} %broadcast_clamp_fusion.2), kind=kCustom, calls=%fused_computation.clone.1 | custom fusion | bytes 4726784 | tf_op jit(solution)/shard_map/while/body/eval_jaxpr/gather | solution.py:100
  317.9 1.1 fusion.54
  319.0 0.3 fusion.55
  319.3 1.2 fusion.56
  320.4 1.4 constant_dynamic-update-slice_fusion.15
  321.8 1.4 constant_dynamic-update-slice_fusion.14
  323.2 1.4 constant_dynamic-update-slice_fusion.13
  324.5 1.4 constant_dynamic-update-slice_fusion.12
  325.9 1.4 constant_dynamic-update-slice_fusion.11
  327.2 1.4 constant_dynamic-update-slice_fusion.10
  328.6 1.4 constant_dynamic-update-slice_fusion.9
  330.0 1.4 constant_dynamic-update-slice_fusion.8
  331.3 1.4 constant_dynamic-update-slice_fusion.7
  332.7 1.4 constant_dynamic-update-slice_fusion.6
  334.1 1.4 constant_dynamic-update-slice_fusion.5
  335.4 1.4 constant_dynamic-update-slice_fusion.4
  336.8 1.4 constant_dynamic-update-slice_fusion.3
  338.2 1.4 constant_dynamic-update-slice_fusion.2
  339.5 1.4 constant_dynamic-update-slice_fusion.1
  340.9 1.4 constant_dynamic-update-slice_fusion
  342.2 45.6 %all-to-all-start.3 = ((bf16[16,4,8,512]{3,2,1,0:T(8,128)(2,1)}), bf16[16,4,8,512]{3,2,1,0:T(8,128)(2,1)S(1)}, u32[]{:S(2)}, u32[]{:S(2)}) async-start(bf16[16,4,8,512]{3,2,1,0:T(8,128)(2,1)} %constant_dynamic-update-slice_fusion), calls=%async_computation.3 | async-start | bytes 1048576 | tf_op jit(solution)/shard_map/all_to_all | solution.py:31
  387.9 0.6 dynamic-slice
  389.1 13.0 %all-to-all-done.3 = bf16[16,4,8,512]{3,2,1,0:T(8,128)(2,1)S(1)} async-done(((bf16[16,4,8,512]{3,2,1,0:T(8,128)(2,1)}), bf16[16,4,8,512]{3,2,1,0:T(8,128)(2,1)S(1)}, u32[]{:S(2)}, u32[]{:S(2)}) %all-to-all-start.3) | async-done | bytes 524320 | tf_op jit(solution)/shard_map/all_to_all | solution.py:31
  402.1 1.6 fusion.20
  403.8 8.0 %fusion.24 = f32[64,7168]{1,0:T(8,128)S(1)} fusion(bf16[1024,7168]{1,0:T(8,128)(2,1)} %param.17, bf16[8,8,8,128]{3,2,1,0:T(8,128)(2,1)S(1)} %fusion.20), kind=kOutput, calls=%fused_computation.37 | convolution fusion | flops 939524096 | bytes 16646144 | tf_op jit(solution)/shard_map/dot_general | solution.py:117
  411.8 73.7 %all-reduce.2 = bf16[64,7168]{1,0:T(8,128)(2,1)} all-reduce(f32[64,7168]{1,0:T(8,128)S(1)} %fusion.24), channel_id=2, replica_groups=mesh['groups'=2,'ctx'=16] {'ctx'}, use_global_device_ids=true, to_apply=%region_9.10.clone | all-reduce | flops 458752 | bytes 2752512
  485.5 1.6 dynamic-slice_convert_fusion
  (62 shorter events, 2.3 us)
Async XLA Ops:
  0.0 38.0 %copy-start = (bf16[8,128,512]{2,1,0:T(8,128)(2,1)S(1)}, bf16[8,128,512]{2,1,0:T(8,128)(2,1)}, u32[]{:S(2)}) copy-start(bf16[8,128,512]{2,1,0:T(8,128)(2,1)} %param.15) | copy-start | bytes 3145732
  2.9 41.1 %all-to-all-start.1 = ((s32[16,1,8]{2,1,0:T(1,128)}), s32[16,1,8]{2,1,0:T(1,128)S(1)}, u32[]{:S(2)}, u32[]{:S(2)}) async-start(s32[16,1,8]{2,1,0:T(1,128)} %bitcast.33), calls=%async_computation.1 | async-start | bytes 16384 | tf_op jit(solution)/shard_map/all_to_all | solution.py:89
  38.6 1.2 copy-start.4
  38.6 1.8 slice-start
  39.8 3.1 slice-start.1
  44.0 20.9 %all-to-all-start = ((bf16[64,8,576]{2,1,0:T(8,128)(2,1)}), bf16[64,8,576]{2,1,0:T(8,128)(2,1)}, u32[]{:S(2)}, u32[]{:S(2)}) async-start(bf16[64,8,576]{2,1,0:T(8,128)(2,1)} %copy.44), calls=%async_computation | async-start | bytes 1310720 | tf_op jit(solution)/shard_map/all_to_all | solution.py:88
  48.2 4.7 copy-start.2
  52.9 1.0 copy-start.3
  64.8 5.2 %copy-start.5 = (s32[4,32]{1,0:T(4,128)S(1)}, s32[4,32]{1,0:T(4,128)}, u32[]{:S(2)}) copy-start(s32[4,32]{1,0:T(4,128)} %param.20) | copy-start | bytes 1540
  64.8 5.5 %copy-start.6 = (s32[4]{0:T(128)S(1)}, s32[4]{0:T(128)}, u32[]{:S(2)}) copy-start(s32[4]{0:T(128)} %param.21) | copy-start | bytes 52
  64.8 192.0 %all-to-all-start.2 = ((bf16[16,8,64,576]{3,2,1,0:T(8,128)(2,1)}), bf16[16,8,64,576]{3,2,1,0:T(8,128)(2,1)}, u32[]{:S(2)}, u32[]{:S(2)}) async-start(bf16[16,8,64,576]{3,2,1,0:T(8,128)(2,1)} %bitcast.94), calls=%async_computation.2 | async-start | bytes 20971520 | tf_op jit(solution)/shard_map/all_to_all | solution.py:90
  256.8 131.1 %copy-start.7 = (u32[32]{0:T(128)S(1)}, u32[32]{0:T(128)}, u32[]{:S(2)}) copy-start(u32[32]{0:T(128)} %constant.72) | copy-start | bytes 388
  342.2 59.9 %all-to-all-start.3 = ((bf16[16,4,8,512]{3,2,1,0:T(8,128)(2,1)}), bf16[16,4,8,512]{3,2,1,0:T(8,128)(2,1)S(1)}, u32[]{:S(2)}, u32[]{:S(2)}) async-start(bf16[16,4,8,512]{3,2,1,0:T(8,128)(2,1)} %constant_dynamic-update-slice_fusion), calls=%async_computation.3 | async-start | bytes 1048576 | tf_op jit(solution)/shard_map/all_to_all | solution.py:31
  403.7 83.3 %copy-start.1 = (bf16[8,128,512]{2,1,0:T(8,128)(2,1)S(1)}, bf16[8,128,512]{2,1,0:T(8,128)(2,1)}, u32[]{:S(2)}) copy-start(bf16[8,128,512]{2,1,0:T(8,128)(2,1)} %param.15) | copy-start | bytes 3145732
